TPU v7x, 32 devices: a whole 2x2x4 slice. The times are simulated.
32 devices in a mesh: section: 8 (over y, x, core), rep: 4 (over z).
Axes of the slice: x: 2, y: 2, z: 4, core: 2. Of those that a mesh axis runs over, the one named last changes fastest.
Arguments:
- features: bfloat16 [16384, 128], P('section'), may hold values from -6 to 6
- order: int32 [16384], P('section'), may hold values from 0 to 2047, as said below
- tiles: bfloat16 [8, 4, 2, 96, 128, 128], P('section', 'rep'), may hold values from -0.125 to 0.125
- tile_rows: int32 [8, 4, 2, 96], P('section', 'rep'), may hold values from 0 to 15, as said below
- tile_cols: int32 [8, 4, 2, 96], P('section', 'rep'), may hold values from 0 to 15, as said below
- live: int32 [8, 4, 2], P('section', 'rep'), may hold values from 1 to 96, as said below
- weight: bfloat16 [128, 128], replicated, may hold values from -0.5 to 0.5
- cotangent: bfloat16 [16384, 128], P('section'), may hold values from -6 to 6
Outputs:
- hidden: bfloat16 [16384, 128], P('section')
- weight_grad: float32 [128, 128], replicated
- feature_grad: bfloat16 [16384, 128], P('section')
Inputs may be any that keep to these rules, and one draw needn't show every extreme that they name: `order`: within each panel of 2048 rows, a permutation of the local row numbers. For one section, replica and round, the 96 pairs (tile_rows, tile_cols) are distinct. `tile_cols`: block column within the panel j * 4 + r for replica r and round j. Some section, replica and round has all 96 slots live.
All inputs are finite; a program needn't handle non-finite values.
Results may differ from a plain program's by a relative error of at most 0.012.
Values may be sent and summed in bfloat16 or wider, within the bound.
No kernel may reach another device: no remote copies, remote signals or barrier semaphores. Data moves between devices by JAX's collectives and lax.ppermute only.
A program may use at most 192 MiB of HBM per device.

v0:
```python
import math
import jax
import jax.numpy as jnp
from jax import lax
from jax.sharding import PartitionSpec as P


def spread(value, axis, source):
    kept = jnp.where(lax.axis_index(axis) == source, value, 0).astype(value.dtype)
    return lax.psum(kept, axis)


def shards(features, order, tiles, tile_rows, tile_cols, live, weight, cotangent):
    rep_count = lax.axis_size("rep")
    section_count = lax.axis_size("section")
    rep_index = lax.axis_index("rep")
    section_index = lax.axis_index("section")
    panel_rows, width = features.shape
    block_rows = tiles.shape[-1]
    blocks = panel_rows // block_rows
    rounds = tiles.shape[2]
    slot_count = tiles.shape[3]
    own_tiles = tiles[0, 0]
    row_table = tile_rows[0, 0]
    col_table = tile_cols[0, 0]
    live_counts = live[0, 0]
    slot_ids = jnp.arange(slot_count, dtype=jnp.int32)
    block_ids = jnp.arange(blocks, dtype=jnp.int32)
    grad_scale = 1.0 / math.sqrt(panel_rows * section_count)
    reordered = jnp.take(features, order, axis=0)

    def forward_round(round_no, running):
        root = round_no * rep_count + rep_index
        panel = spread(reordered, "section", root)
        tile_set = lax.dynamic_index_in_dim(own_tiles, round_no, 0, keepdims=False)
        row_ids = lax.dynamic_index_in_dim(row_table, round_no, 0, keepdims=False)
        col_ids = lax.dynamic_index_in_dim(col_table, round_no, 0, keepdims=False)
        count_now = lax.dynamic_index_in_dim(live_counts, round_no, 0, keepdims=False)
        picked = jnp.take(panel.reshape(blocks, block_rows, width), col_ids, axis=0)
        products = jnp.einsum("kab,kbf->kaf", tile_set, picked, preferred_element_type=jnp.float32)
        select = (
            (row_ids[None, :] == block_ids[:, None]) & (slot_ids < count_now)[None, :]
        ).astype(jnp.float32)
        return running + jnp.einsum(
            "pk,kaf->paf", select, products, precision=lax.Precision.HIGHEST
        )

    partial_sum = lax.fori_loop(
        0, rounds, forward_round, jnp.zeros((blocks, block_rows, width), jnp.float32)
    )
    partial_sum = partial_sum.reshape(panel_rows, width)
    share_rows = panel_rows // rep_count
    row_share = lax.psum_scatter(partial_sum, "rep", scatter_dimension=0, tiled=True)
    co_share = lax.dynamic_slice_in_dim(cotangent, rep_index * share_rows, share_rows, 0)
    aggregated = row_share.astype(jnp.bfloat16)
    preact = jnp.dot(aggregated, weight, preferred_element_type=jnp.float32)
    out_rows = jax.nn.silu(preact).astype(jnp.bfloat16)
    sigmoid_part = jax.nn.sigmoid(preact)
    grad_pre = (
        co_share.astype(jnp.float32) * sigmoid_part * (1.0 + preact * (1.0 - sigmoid_part))
    ).astype(jnp.bfloat16)
    grad_part = jnp.einsum("nf,ng->fg", aggregated, grad_pre, preferred_element_type=jnp.float32)
    up_rows = jnp.einsum("ng,fg->nf", grad_pre, weight, preferred_element_type=jnp.float32).astype(
        jnp.bfloat16
    )
    hidden_share, grad_part, upstream_share = (out_rows, grad_part, up_rows)
    weight_grad = lax.psum(grad_part, ("section", "rep")) * grad_scale
    hidden, upstream = (
        lax.all_gather(hidden_share, "rep", axis=0, tiled=True),
        lax.all_gather(upstream_share, "rep", axis=0, tiled=True),
    )
    up_blocks = upstream.reshape(blocks, block_rows, width)
    picked_up = jnp.take(up_blocks, row_table.reshape(-1), axis=0).reshape(
        rounds, slot_count, block_rows, width
    )
    products_back = jnp.einsum(
        "jkab,jkaf->jkbf", own_tiles, picked_up, preferred_element_type=jnp.float32
    )
    alive_mask = slot_ids[None, None, :] < live_counts[:, None, None]
    select_back = ((col_table[:, None, :] == block_ids[None, :, None]) & alive_mask).astype(
        jnp.float32
    )
    contrib = jnp.einsum(
        "jpk,jkbf->jpbf", select_back, products_back, precision=lax.Precision.HIGHEST
    )
    contrib = lax.optimization_barrier(contrib.astype(jnp.bfloat16)).astype(jnp.float32)
    contrib = contrib.reshape(rounds, panel_rows, width)
    totals = lax.psum(contrib.astype(jnp.bfloat16), "section").astype(jnp.float32)
    own_panel = lax.dynamic_index_in_dim(
        totals, section_index // rep_count, 0, keepdims=False
    ).astype(jnp.bfloat16)
    grad_rows = spread(own_panel, "rep", section_index % rep_count)
    feature_grad = jnp.zeros_like(features).at[order].set(grad_rows)
    return (hidden, weight_grad, feature_grad)


def solution(mesh):
    placed = (
        P("section", None),
        P("section"),
        P("section", "rep", None, None, None, None),
        P("section", "rep", None, None),
        P("section", "rep", None, None),
        P("section", "rep", None),
        P(),
        P("section", None),
    )
    return jax.shard_map(
        shards,
        mesh=mesh,
        in_specs=placed,
        out_specs=(P("section", None), P(), P("section", None)),
        check_vma=False,
    )
```

profile of v0, /device:TPU:0, one launch (start us, length us, event | category | flops | bytes accessed | tf_op | source)
XLA Modules:
  0.0 487.0 jit_solution(13288153377587932532)
XLA Ops:
  9.5 6.2 %gather_fusion.1 = bf16[2048,128]{1,0:T(8,128)(2,1)S(1)} fusion(bf16[2048,128]{1,0:T(8,128)(2,1)S(1)} %copy-done, s32[2048]{0:T(1024)S(1)} %get-tuple-element.296), kind=kCustom, calls=%fused_computation.1 | custom fusion | bytes 1056768 | tf_op jit(solution)/shard_map/jit(_take)/gather | solution.py:30
  16.0 147.6 %while.16 = (s32[]{:T(128)}, f32[16,128,128]{2,0,1:T(8,128)S(1)}, s32[2,96]{1,0:T(2,128)}, s32[2]{0:T(128)}, bf16[2,96,128,128]{3,2,1,0:T(8,128)(2,1)}, /*index=...) while((s32[]{:T(128)}, f32[16,128,128]{2,0,1:T(8,128)S(1)}, ...), condition=%wide.region_2.3_spmd.clone, body=%wide.region_0.0_spmd.clone.sunk | while | flops 707269568 | bytes 31465112 | solution.py:48
  16.1 0.8 broadcast_select_fusion.3
  18.3 1.2 dynamic_slice.80
  20.9 57.2 %all-reduce.11.cloned.1.call-done = bf16[16,128,128]{2,1,0:T(8,128)(2,1)} async-done(((bf16[16,128,128]{2,1,0:T(8,128)(2,1)}), bf16[16,128,128]{2,1,0:T(8,128)(2,1)}) %all-reduce.11.cloned.1.call-update) | async-done | bytes 524304 | tf_op jit(solution)/shard_map/while/body/eval_jaxpr/psum | solution.py:10
  78.1 3.7 gather_fusion
  81.9 3.9 fusion.65
  85.8 5.7 %fusion.67 = f32[16,128,128]{2,0,1:T(8,128)S(1)} fusion(f32[96,128,128]{2,1,0:T(8,128)S(1)} %fusion.65, f32[16,128,128]{2,0,1:T(8,128)S(1)} %get-tuple-element.360, pred[]{:T(512)S(6)} %compare.6, s32[96]{0:T(128)S(1)} %fusion.66, pred[96]{0:T(512)(128)(4,1)S(1)} %iota_compare_fusion.5), kind=kOutput, calls=%fused_computation.14.clone.1 | convolution fusion | flops 302517248 | bytes 8389089 | tf_op jit(solution)/shard_map/while/body/eval_jaxpr/pk,kaf->paf/dot_general | solution.py:44
  91.6 0.8 broadcast_select_fusion.3
  93.8 1.2 dynamic_slice.80
  96.4 53.8 %all-reduce.11.cloned.1.call-done = bf16[16,128,128]{2,1,0:T(8,128)(2,1)} async-done(((bf16[16,128,128]{2,1,0:T(8,128)(2,1)}), bf16[16,128,128]{2,1,0:T(8,128)(2,1)}) %all-reduce.11.cloned.1.call-update) | async-done | bytes 524304 | tf_op jit(solution)/shard_map/while/body/eval_jaxpr/psum | solution.py:10
  150.2 3.7 gather_fusion
  154.0 3.9 fusion.65
  157.9 5.7 %fusion.67 = f32[16,128,128]{2,0,1:T(8,128)S(1)} fusion(f32[96,128,128]{2,1,0:T(8,128)S(1)} %fusion.65, f32[16,128,128]{2,0,1:T(8,128)S(1)} %get-tuple-element.360, pred[]{:T(512)S(6)} %compare.6, s32[96]{0:T(128)S(1)} %fusion.66, pred[96]{0:T(512)(128)(4,1)S(1)} %iota_compare_fusion.5), kind=kOutput, calls=%fused_computation.14.clone.1 | convolution fusion | flops 302517248 | bytes 8389089 | tf_op jit(solution)/shard_map/while/body/eval_jaxpr/pk,kaf->paf/dot_general | solution.py:44
  163.7 1.3 copy.11
  167.3 25.6 %reduce-scatter.2.cloned.1.call-done = f32[512,128]{1,0:T(8,128)} async-done(((f32[2048,128]{1,0:T(8,128)}), f32[512,128]{1,0:T(8,128)}) %reduce-scatter.2.cloned.1.call-update) | async-done | bytes 262160 | tf_op jit(solution)/shard_map/reduce_scatter | solution.py:53
  192.9 1.3 multiply_convert_fusion
  194.3 16.2 %all_gather.7 = bf16[2048,128]{1,0:T(8,128)(2,1)S(1)} all-gather(bf16[512,128]{1,0:T(8,128)(2,1)S(1)} %convolution_convert_fusion), channel_id=1, replica_groups=mesh['section'=8,'rep'=4] {'rep'}, dimensions={0}, use_global_device_ids=true | all-gather | bytes 655360 | tf_op jit(solution)/shard_map/all_gather | solution.py:70
  210.5 8.0 %gather_fusion.2 = bf16[192,128,128]{2,1,0:T(8,128)(2,1)} fusion(bf16[16,128,128]{2,1,0:T(8,128)(2,1)S(1)} %bitcast.60, s32[1024]{0:T(1024)S(1)} %pad_clamp_fusion.1), kind=kCustom, calls=%fused_computation.2 | custom fusion | bytes 12583680 | tf_op jit(solution)/shard_map/jit(_take)/gather | solution.py:73
  218.5 11.6 %fusion.26 = f32[2,96,128,128]{3,2,1,0:T(8,128)} fusion(bf16[2,96,128,128]{3,2,1,0:T(8,128)(2,1)} %bitcast.64, pred[2,96]{1,0:T(4,128)(4,1)S(1)} %compare_and_fusion.2, bf16[1,1,2,96,128,128]{5,4,3,2,1,0:T(8,128)(2,1)} %bitcast.62), kind=kOutput, calls=%fused_computation.34 | convolution fusion | flops 808452096 | bytes 25166016 | tf_op jit(solution)/shard_map/jkab,jkaf->jkbf/dot_general | solution.py:76
  230.1 12.8 %copy.14 = f32[2,96,128,128]{2,1,3,0:T(8,128)} copy(f32[2,96,128,128]{3,2,1,0:T(8,128)} %fusion.26) | data formatting | bytes 25165824 | tf_op jit(solution)/shard_map/jkab,jkaf->jkbf/dot_general | solution.py:76
  242.8 7.2 %fusion.30 = bf16[2,16,128,128]{3,1,2,0:T(8,128)(2,1)S(1)} fusion(f32[2,96,128,128]{2,1,3,0:T(8,128)} %copy.14, s32[2,96]{1,0:T(2,128)S(1)} %copy-done.3, pred[2,96]{1,0:T(4,128)(4,1)S(1)} %iota_compare_fusion.3), kind=kOutput, calls=%fused_computation.38 | convolution fusion | flops 604510208 | bytes 13632448 | tf_op jit(solution)/shard_map/jpk,jkbf->jpbf/dot_general | solution.py:83
  250.1 1.3 copy.12
  251.5 0.9 fusion.37
  252.5 53.3 %all-reduce.7.cloned.1.call-done = bf16[2,2048,128]{2,1,0:T(8,128)(2,1)} async-done(((bf16[2,2048,128]{2,1,0:T(8,128)(2,1)}), bf16[2,2048,128]{2,1,0:T(8,128)(2,1)}) %all-reduce.7.cloned.1.call-update) | async-done | bytes 1048592 | tf_op jit(solution)/shard_map/psum | solution.py:88
  305.8 1.9 fusion.34
  307.7 14.8 %all_gather.6 = bf16[2048,128]{1,0:T(8,128)(2,1)S(1)} all-gather(bf16[512,128]{1,0:T(8,128)(2,1)S(1)} %get-tuple-element.294), channel_id=1, replica_groups=mesh['section'=8,'rep'=4] {'rep'}, dimensions={0}, use_global_device_ids=true | all-gather | bytes 655360 | tf_op jit(solution)/shard_map/all_gather | solution.py:69
  322.5 106.7 %all-reduce.5.cloned.1.call-done = f32[128,128]{1,0:T(8,128)} async-done(((f32[128,128]{1,0:T(8,128)}), f32[128,128]{1,0:T(8,128)}) %all-reduce.5.cloned.1.call-update) | async-done | bytes 65552 | tf_op jit(solution)/shard_map/psum | solution.py:67
  429.3 1.5 broadcast_multiply_fusion
  430.7 41.1 %all-reduce.9.cloned.1.call-done = bf16[2048,128]{1,0:T(8,128)(2,1)} async-done(((bf16[2048,128]{1,0:T(8,128)(2,1)}), bf16[2048,128]{1,0:T(8,128)(2,1)}) %all-reduce.9.cloned.1.call-update) | async-done | bytes 524304 | tf_op jit(solution)/shard_map/psum | solution.py:10
  471.8 6.8 %scatter_custom_fusion = bf16[2048,128]{1,0:T(8,128)(2,1)} fusion(s32[2048]{0:T(1024)S(1)} %get-tuple-element.295, bf16[2048,128]{1,0:T(8,128)(2,1)} %all-reduce.9.cloned.1.call-done, bf16[]{:T(256)} %constant.190.clone.1), kind=kCustom, calls=%fused_computation.44 | custom fusion | bytes 524800 | tf_op jit(solution)/shard_map/scatter | solution.py:93
  478.7 0.8 copy.33
  (40 shorter events, 10.0 us)
Async XLA Ops:
  8.0 1.5 copy-start
  16.0 176.9 %copy-start.2 = (bf16[128,128]{1,0:T(8,128)(2,1)S(1)}, bf16[128,128]{1,0:T(8,128)(2,1)}, u32[]{:S(2)}) copy-start(bf16[128,128]{1,0:T(8,128)(2,1)} %param.16) | copy-start | bytes 98308
  16.0 62.1 %all-reduce.11.cloned.1.call-start = ((), (), s32[]{:S(2)}) async-start(), calls=%async_computation.5 | async-start | bytes 1048576 | tf_op jit(solution)/shard_map/while/body/eval_jaxpr/psum | solution.py:10
  91.5 58.7 %all-reduce.11.cloned.1.call-start = ((), (), s32[]{:S(2)}) async-start(), calls=%async_computation.5 | async-start | bytes 1048576 | tf_op jit(solution)/shard_map/while/body/eval_jaxpr/psum | solution.py:10
  163.6 29.2 %reduce-scatter.2.cloned.1.call-start = ((), (), s32[]{:S(2)}) async-start(), calls=%async_computation.1 | async-start | bytes 1310720 | tf_op jit(solution)/shard_map/reduce_scatter | solution.py:53
  165.0 140.7 %all-reduce.7.cloned.1.call-start = ((), (), s32[]{:S(2)}) async-start(), calls=%async_computation.3 | async-start | bytes 2097152 | tf_op jit(solution)/shard_map/psum | solution.py:88
  230.1 12.8 %copy-start.3 = (s32[2,96]{1,0:T(2,128)S(1)}, s32[2,96]{1,0:T(2,128)}, u32[]{:S(2)}) copy-start(s32[2,96]{1,0:T(2,128)} %get-tuple-element.411) | copy-start | bytes 2308
  242.8 8.7 %copy-start.1 = (f32[512,128]{1,0:T(8,128)S(1)}, f32[512,128]{1,0:T(8,128)}, u32[]{:S(2)}) copy-start(f32[512,128]{1,0:T(8,128)} %reduce-scatter.2.cloned.1.call-done) | copy-start | bytes 786436
  251.4 177.8 %all-reduce.5.cloned.1.call-start = ((), (), s32[]{:S(2)}) async-start(), calls=%async_computation.2 | async-start | bytes 131072 | tf_op jit(solution)/shard_map/psum | solution.py:67
  252.4 219.4 %all-reduce.9.cloned.1.call-start = ((), (), s32[]{:S(2)}) async-start(), calls=%async_computation.4 | async-start | bytes 1048576 | tf_op jit(solution)/shard_map/psum | solution.py:10
Sparse Core Ops, SparseCore 0:
  20.8 57.2 all-reduce.10
  96.3 53.8 all-reduce.10
Sparse Core Ops, SparseCore 1:
  166.4 26.4 reduce-scatter.1
  251.5 54.2 all-reduce.6
  312.7 116.5 all-reduce.4
  432.3 39.4 all-reduce.8
where the time goes:
time: 488 us; the launch traced here: 487 us
  waiting for transfers between devices  338 us (69%)
  local copies, waits for them, and re-layouts  49.3 us (10%)
  matrix products  40.4 us (8%)
  blocking collectives  31 us (6%)
  between operations  15.8 us (3%)
  other arithmetic  12.4 us (3%)
    psum x3, waiting for transfers between devices, spread(): return lax.psum(kept, axis)  152 us
    psum x1, waiting for transfers between devices, shards(): weight_grad = lax.psum(grad_part, ('section', 'rep')) * grad_scale  107 us
    psum x1, waiting for transfers between devices, shards(): lax.psum(contrib.astype(jnp.bfloat16), 'section').astype(jnp.float32)  53.3 us
    reduce_scatter x1, waiting for transfers between devices, shards(): lax.psum_scatter(partial_sum, 'rep', scatter_dimension=0, tiled=True)  25.6 us
    all_gather x1, blocking collectives, shards(): lax.all_gather(upstream_share, 'rep', axis=0, tiled=True)  16.2 us
    all_gather x1, blocking collectives, shards(): lax.all_gather(hidden_share, 'rep', axis=0, tiled=True)  14.8 us
    dot_general x1, local copies, waits for them, and re-layouts, shards(): jnp.einsum('jkab,jkaf->jkbf', own_tiles, picked_up, preferred_element_typ...  12.8 us
    dot_general x1, matrix products, shards(): jnp.einsum('jkab,jkaf->jkbf', own_tiles, picked_up, preferred_element_typ...  11.6 us
  transfers between devices with their start and end apart: 6, of which 6 were waited for; matrix products, arithmetic and copies ran while one was open for 3% of the time, Pallas kernels for 0%

commit v1 on v0

--- a/solution.py
+++ b/solution.py
@@ -64,7 +64,7 @@
         jnp.bfloat16
     )
     hidden_share, grad_part, upstream_share = (out_rows, grad_part, up_rows)
-    weight_grad = lax.psum(grad_part, ("section", "rep")) * grad_scale
+    weight_grad = jnp.sum(lax.all_gather(grad_part, ("section", "rep")), axis=0) * grad_scale
     hidden, upstream = (
         lax.all_gather(hidden_share, "rep", axis=0, tiled=True),
         lax.all_gather(upstream_share, "rep", axis=0, tiled=True),

time: 488 us -> 421 us (0.86)
  waiting for transfers between devices: 338 us -> 263 us
  blocking collectives: 31 us -> 38.2 us
    psum x1 -> x0, waiting for transfers between devices: 107 us -> none  [shards(): weight_grad = lax.psum(grad_part, ('section', 'rep')) * grad_scale]
    all_gather x0 -> x1, waiting for transfers between devices: none -> 53 us  [shards(): lax.all_gather(grad_part, ('section', 'rep'))]
    psum x3, waiting for transfers between devices: 152 us -> 130 us  [spread(): return lax.psum(kept, axis)]
    all_gather x1, blocking collectives: 14.8 us -> 22 us  [shards(): lax.all_gather(hidden_share, 'rep', axis=0, tiled=True)]
  transfers between devices with their start and end apart: 6 -> 6, of which waited for: 6 -> 6; matrix products, arithmetic and copies ran while one was open for 3% -> 4% of each run, Pallas kernels for 0% -> 0%
where the time goes in v1:
time: 421 us; the launch traced here: 420 us
  waiting for transfers between devices  263 us (62%)
  local copies, waits for them, and re-layouts  49.3 us (12%)
  matrix products  40.4 us (10%)
  blocking collectives  38.2 us (9%)
  between operations  15.8 us (4%)
  other arithmetic  13.2 us (3%)
    psum x3, waiting for transfers between devices, spread(): return lax.psum(kept, axis)  130 us
    psum x1, waiting for transfers between devices, shards(): lax.psum(contrib.astype(jnp.bfloat16), 'section').astype(jnp.float32)  54.2 us
    all_gather x1, waiting for transfers between devices, shards(): lax.all_gather(grad_part, ('section', 'rep'))  53 us
    reduce_scatter x1, waiting for transfers between devices, shards(): lax.psum_scatter(partial_sum, 'rep', scatter_dimension=0, tiled=True)  25.6 us
    all_gather x1, blocking collectives, shards(): lax.all_gather(hidden_share, 'rep', axis=0, tiled=True)  22 us
    all_gather x1, blocking collectives, shards(): lax.all_gather(upstream_share, 'rep', axis=0, tiled=True)  16.2 us
    dot_general x1, local copies, waits for them, and re-layouts, shards(): jnp.einsum('jkab,jkaf->jkbf', own_tiles, picked_up, preferred_element_typ...  12.8 us
    dot_general x1, matrix products, shards(): jnp.einsum('jkab,jkaf->jkbf', own_tiles, picked_up, preferred_element_typ...  11.6 us
  transfers between devices with their start and end apart: 6, of which 6 were waited for; matrix products, arithmetic and copies ran while one was open for 4% of the time, Pallas kernels for 0%

profile of v1, /device:TPU:0, one launch (start us, length us, event | category | flops | bytes accessed | tf_op | source)
XLA Modules:
  0.0 420.0 jit_solution(7098529603962226911)
XLA Ops:
  9.5 6.2 %gather_fusion.1 = bf16[2048,128]{1,0:T(8,128)(2,1)S(1)} fusion(bf16[2048,128]{1,0:T(8,128)(2,1)S(1)} %copy-done, s32[2048]{0:T(1024)S(1)} %get-tuple-element.296), kind=kCustom, calls=%fused_computation.1 | custom fusion | bytes 1056768 | tf_op jit(solution)/shard_map/jit(_take)/gather | solution.py:30
  16.0 147.6 %while.16 = (s32[]{:T(128)}, f32[16,128,128]{2,0,1:T(8,128)S(1)}, s32[2,96]{1,0:T(2,128)}, s32[2]{0:T(128)}, bf16[2,96,128,128]{3,2,1,0:T(8,128)(2,1)}, /*index=...) while((s32[]{:T(128)}, f32[16,128,128]{2,0,1:T(8,128)S(1)}, ...), condition=%wide.region_2.3_spmd.clone, body=%wide.region_0.0_spmd.clone.sunk | while | flops 707269568 | bytes 31465112 | solution.py:48
  16.1 0.8 broadcast_select_fusion.3
  18.3 1.2 dynamic_slice.80
  20.9 57.2 %all-reduce.8.cloned.1.call-done = bf16[16,128,128]{2,1,0:T(8,128)(2,1)} async-done(((bf16[16,128,128]{2,1,0:T(8,128)(2,1)}), bf16[16,128,128]{2,1,0:T(8,128)(2,1)}) %all-reduce.8.cloned.1.call-update) | async-done | bytes 524304 | tf_op jit(solution)/shard_map/while/body/eval_jaxpr/psum | solution.py:10
  78.1 3.7 gather_fusion
  81.9 3.9 fusion.65
  85.8 5.7 %fusion.67 = f32[16,128,128]{2,0,1:T(8,128)S(1)} fusion(f32[96,128,128]{2,1,0:T(8,128)S(1)} %fusion.65, f32[16,128,128]{2,0,1:T(8,128)S(1)} %get-tuple-element.360, pred[]{:T(512)S(6)} %compare.6, s32[96]{0:T(128)S(1)} %fusion.66, pred[96]{0:T(512)(128)(4,1)S(1)} %iota_compare_fusion.5), kind=kOutput, calls=%fused_computation.14.clone.1 | convolution fusion | flops 302517248 | bytes 8389089 | tf_op jit(solution)/shard_map/while/body/eval_jaxpr/pk,kaf->paf/dot_general | solution.py:44
  91.6 0.8 broadcast_select_fusion.3
  93.8 1.2 dynamic_slice.80
  96.4 53.8 %all-reduce.8.cloned.1.call-done = bf16[16,128,128]{2,1,0:T(8,128)(2,1)} async-done(((bf16[16,128,128]{2,1,0:T(8,128)(2,1)}), bf16[16,128,128]{2,1,0:T(8,128)(2,1)}) %all-reduce.8.cloned.1.call-update) | async-done | bytes 524304 | tf_op jit(solution)/shard_map/while/body/eval_jaxpr/psum | solution.py:10
  150.2 3.7 gather_fusion
  154.0 3.9 fusion.65
  157.9 5.7 %fusion.67 = f32[16,128,128]{2,0,1:T(8,128)S(1)} fusion(f32[96,128,128]{2,1,0:T(8,128)S(1)} %fusion.65, f32[16,128,128]{2,0,1:T(8,128)S(1)} %get-tuple-element.360, pred[]{:T(512)S(6)} %compare.6, s32[96]{0:T(128)S(1)} %fusion.66, pred[96]{0:T(512)(128)(4,1)S(1)} %iota_compare_fusion.5), kind=kOutput, calls=%fused_computation.14.clone.1 | convolution fusion | flops 302517248 | bytes 8389089 | tf_op jit(solution)/shard_map/while/body/eval_jaxpr/pk,kaf->paf/dot_general | solution.py:44
  163.7 1.3 copy.11
  167.3 25.6 %reduce-scatter.2.cloned.1.call-done = f32[512,128]{1,0:T(8,128)} async-done(((f32[2048,128]{1,0:T(8,128)}), f32[512,128]{1,0:T(8,128)}) %reduce-scatter.2.cloned.1.call-update) | async-done | bytes 262160 | tf_op jit(solution)/shard_map/reduce_scatter | solution.py:53
  192.9 1.3 multiply_convert_fusion
  194.3 16.2 %all_gather.15 = bf16[2048,128]{1,0:T(8,128)(2,1)S(1)} all-gather(bf16[512,128]{1,0:T(8,128)(2,1)S(1)} %convolution_convert_fusion), channel_id=1, replica_groups=mesh['section'=8,'rep'=4] {'rep'}, dimensions={0}, use_global_device_ids=true | all-gather | bytes 655360 | tf_op jit(solution)/shard_map/all_gather | solution.py:70
  210.5 8.0 %gather_fusion.2 = bf16[192,128,128]{2,1,0:T(8,128)(2,1)} fusion(bf16[16,128,128]{2,1,0:T(8,128)(2,1)S(1)} %bitcast.61, s32[1024]{0:T(1024)S(1)} %pad_clamp_fusion.1), kind=kCustom, calls=%fused_computation.2 | custom fusion | bytes 12583680 | tf_op jit(solution)/shard_map/jit(_take)/gather | solution.py:73
  218.5 11.6 %fusion.26 = f32[2,96,128,128]{3,2,1,0:T(8,128)} fusion(bf16[2,96,128,128]{3,2,1,0:T(8,128)(2,1)} %bitcast.65, pred[2,96]{1,0:T(4,128)(4,1)S(1)} %compare_and_fusion.2, bf16[1,1,2,96,128,128]{5,4,3,2,1,0:T(8,128)(2,1)} %bitcast.63), kind=kOutput, calls=%fused_computation.34 | convolution fusion | flops 808452096 | bytes 25166016 | tf_op jit(solution)/shard_map/jkab,jkaf->jkbf/dot_general | solution.py:76
  230.1 12.8 %copy.14 = f32[2,96,128,128]{2,1,3,0:T(8,128)} copy(f32[2,96,128,128]{3,2,1,0:T(8,128)} %fusion.26) | data formatting | bytes 25165824 | tf_op jit(solution)/shard_map/jkab,jkaf->jkbf/dot_general | solution.py:76
  242.8 7.2 %fusion.30 = bf16[2,16,128,128]{3,1,2,0:T(8,128)(2,1)S(1)} fusion(f32[2,96,128,128]{2,1,3,0:T(8,128)} %copy.14, s32[2,96]{1,0:T(2,128)S(1)} %copy-done.3, pred[2,96]{1,0:T(4,128)(4,1)S(1)} %iota_compare_fusion.3), kind=kOutput, calls=%fused_computation.38 | convolution fusion | flops 604510208 | bytes 13632448 | tf_op jit(solution)/shard_map/jpk,jkbf->jpbf/dot_general | solution.py:83
  250.1 1.3 copy.12
  251.5 54.2 %all-reduce.4.cloned.1.call-done = bf16[2,2048,128]{2,1,0:T(8,128)(2,1)} async-done(((bf16[2,2048,128]{2,1,0:T(8,128)(2,1)}), bf16[2,2048,128]{2,1,0:T(8,128)(2,1)}) %all-reduce.4.cloned.1.call-update) | async-done | bytes 1048592 | tf_op jit(solution)/shard_map/psum | solution.py:88
  305.8 1.9 fusion.34
  307.8 0.9 fusion.37
  308.7 22.0 %all_gather.12 = bf16[2048,128]{1,0:T(8,128)(2,1)S(1)} all-gather(bf16[512,128]{1,0:T(8,128)(2,1)S(1)} %get-tuple-element.294), channel_id=1, replica_groups=mesh['section'=8,'rep'=4] {'rep'}, dimensions={0}, use_global_device_ids=true | all-gather | bytes 655360 | tf_op jit(solution)/shard_map/all_gather | solution.py:69
  330.7 18.7 %all-reduce.6.cloned.1.call-done = bf16[2048,128]{1,0:T(8,128)(2,1)} async-done(((bf16[2048,128]{1,0:T(8,128)(2,1)}), bf16[2048,128]{1,0:T(8,128)(2,1)}) %all-reduce.6.cloned.1.call-update) | async-done | bytes 524304 | tf_op jit(solution)/shard_map/psum | solution.py:10
  349.4 6.8 %scatter_custom_fusion = bf16[2048,128]{1,0:T(8,128)(2,1)} fusion(s32[2048]{0:T(1024)S(1)} %get-tuple-element.295, bf16[2048,128]{1,0:T(8,128)(2,1)} %all-reduce.6.cloned.1.call-done, bf16[]{:T(256)} %constant.191.clone.1), kind=kCustom, calls=%fused_computation.44 | custom fusion | bytes 524800 | tf_op jit(solution)/shard_map/scatter | solution.py:93
  356.2 53.0 %all-gather.3.cloned.1.call-done = f32[4096,128]{1,0:T(8,128)} async-done(((f32[128,128]{1,0:T(8,128)}), f32[4096,128]{1,0:T(8,128)}) %all-gather.3.cloned.1.call-update) | async-done | bytes 2097168 | tf_op jit(solution)/shard_map/all_gather | solution.py:67
  409.3 1.7 reduce_sum.9
  411.6 0.8 copy.32
  (41 shorter events, 10.6 us)
Async XLA Ops:
  8.0 1.5 copy-start
  16.0 176.9 %copy-start.2 = (bf16[128,128]{1,0:T(8,128)(2,1)S(1)}, bf16[128,128]{1,0:T(8,128)(2,1)}, u32[]{:S(2)}) copy-start(bf16[128,128]{1,0:T(8,128)(2,1)} %param.16) | copy-start | bytes 98308
  16.0 62.1 %all-reduce.8.cloned.1.call-start = ((), (), s32[]{:S(2)}) async-start(), calls=%async_computation.5 | async-start | bytes 1048576 | tf_op jit(solution)/shard_map/while/body/eval_jaxpr/psum | solution.py:10
  91.5 58.7 %all-reduce.8.cloned.1.call-start = ((), (), s32[]{:S(2)}) async-start(), calls=%async_computation.5 | async-start | bytes 1048576 | tf_op jit(solution)/shard_map/while/body/eval_jaxpr/psum | solution.py:10
  163.6 29.2 %reduce-scatter.2.cloned.1.call-start = ((), (), s32[]{:S(2)}) async-start(), calls=%async_computation.1 | async-start | bytes 1310720 | tf_op jit(solution)/shard_map/reduce_scatter | solution.py:53
  165.0 140.7 %all-reduce.4.cloned.1.call-start = ((), (), s32[]{:S(2)}) async-start(), calls=%async_computation.2 | async-start | bytes 2097152 | tf_op jit(solution)/shard_map/psum | solution.py:88
  230.1 12.8 %copy-start.3 = (s32[2,96]{1,0:T(2,128)S(1)}, s32[2,96]{1,0:T(2,128)}, u32[]{:S(2)}) copy-start(s32[2,96]{1,0:T(2,128)} %get-tuple-element.411) | copy-start | bytes 2308
  242.8 64.9 %copy-start.1 = (f32[512,128]{1,0:T(8,128)S(1)}, f32[512,128]{1,0:T(8,128)}, u32[]{:S(2)}) copy-start(f32[512,128]{1,0:T(8,128)} %reduce-scatter.2.cloned.1.call-done) | copy-start | bytes 786436
  251.4 98.0 %all-reduce.6.cloned.1.call-start = ((), (), s32[]{:S(2)}) async-start(), calls=%async_computation.3 | async-start | bytes 1048576 | tf_op jit(solution)/shard_map/psum | solution.py:10
  307.7 101.6 %all-gather.3.cloned.1.call-start = ((), (), s32[]{:S(2)}) async-start(), calls=%async_computation.4 | async-start | bytes 2162688 | tf_op jit(solution)/shard_map/all_gather | solution.py:67
Sparse Core Ops, SparseCore 0:
  20.8 57.2 all-reduce.7
  96.3 53.8 all-reduce.7
Sparse Core Ops, SparseCore 1:
  166.4 26.4 reduce-scatter.1
  251.5 54.2 all-reduce.3
  308.7 40.7 all-reduce.5
  353.4 55.9 all-gather.2
